TPU v7x, 512 devices: a whole 4x8x8 slice. The times are simulated.
512 devices in a mesh: row: 16 (over y, core), col: 32 (over z, x).
Axes of the slice: x: 4, y: 8, z: 8, core: 2. Of those that a mesh axis runs over, the one named last changes fastest.
Arguments:
- surface: float32 [2, 1024, 4096], P(None, 'row', 'col'), may hold values from -0.5 to 0.5
- u_face: float32 [2, 1024, 4096], P(None, 'row', 'col'), may hold values from -3 to 3
- v_face: float32 [2, 1024, 4096], P(None, 'row', 'col'), may hold values from -3 to 3
- bed_depth: float32 [1024, 4096], P('row', 'col'), may hold values from 1 to 10
- wet_mask: int32 [2, 1024, 4096], P(None, 'row', 'col'), may hold values 0 or 1
- rainfall: float32 [2, 1024, 4096], P(None, 'row', 'col'), may hold values from 0.05 to 0.5
Outputs:
- new_surface: float32 [2, 1024, 4096], P(None, 'row', 'col')
- new_u: float32 [2, 1024, 4096], P(None, 'row', 'col')
- new_v: float32 [2, 1024, 4096], P(None, 'row', 'col')
All inputs are finite; a program needn't handle non-finite values. No bound on the sum of `wet_mask` on one device may be relied on, other than what follows from the above.
Results may differ from a plain program's by a relative error of at most 0.0003.
Values sent between devices are 32-bit elements; how exact they have to be, the bound alone decides.
A program may use at most 64 MiB of HBM per device.

v0:
```python
import jax
import jax.numpy as jnp
from jax import lax
from jax.sharding import PartitionSpec as P

ITERS = 3
DTDX = 0.5
FRIC = 0.05
G1 = 4.0
CK = DTDX * G1


def extended(cells, sides, width):
    for axis, dim in sides:
        count = lax.axis_size(axis)
        ends = count - 1
        head = lax.slice_in_dim(cells, 0, width, axis=dim)
        tail = lax.slice_in_dim(cells, cells.shape[dim] - width, cells.shape[dim], axis=dim)
        cells = jnp.concatenate(
            [
                lax.ppermute(tail, axis, [(i, (i + 1) % count) for i in range(ends)]),
                cells,
                lax.ppermute(head, axis, [((i + 1) % count, i) for i in range(ends)]),
            ],
            axis=dim,
        )
    return cells


def passed_along(block, axis, distance):
    devices = range(lax.axis_size(axis))
    route = [(i - distance, i) for i in devices if i - distance in devices]
    return lax.ppermute(block, axis, route)


def explicit(eta2, u2, v2, dep2, wet2, ny, nx):

    def view(a, dy, dx):
        return a[:, 1 + dy : 3 + dy + ny, 1 + dx : 3 + dx + nx]

    h_here = view(eta2, 0, 0) + view(dep2, 0, 0)
    h_east = view(eta2, 0, 1) + view(dep2, 0, 1)
    h_north = view(eta2, 1, 0) + view(dep2, 1, 0)
    wet_x = view(wet2, 0, 0) * view(wet2, 0, 1)
    wet_y = view(wet2, 0, 0) * view(wet2, 1, 0)
    depth_x = 0.5 * (h_here + h_east)
    depth_y = 0.5 * (h_here + h_north)
    u_here = view(u2, 0, 0)
    v_here = view(v2, 0, 0)
    v_mean = 0.25 * (v_here + view(v2, 0, 1) + view(v2, -1, 0) + view(v2, -1, 1))
    u_mean = 0.25 * (u_here + view(u2, 0, -1) + view(u2, 1, 0) + view(u2, 1, -1))
    adv_u = jnp.where(
        u_here > 0, u_here * (u_here - view(u2, 0, -1)), u_here * (view(u2, 0, 1) - u_here)
    )
    adv_u = adv_u + jnp.where(
        v_mean > 0, v_mean * (u_here - view(u2, -1, 0)), v_mean * (view(u2, 1, 0) - u_here)
    )
    adv_v = jnp.where(
        v_here > 0, v_here * (v_here - view(v2, -1, 0)), v_here * (view(v2, 1, 0) - v_here)
    )
    adv_v = adv_v + jnp.where(
        u_mean > 0, u_mean * (v_here - view(v2, 0, -1)), u_mean * (view(v2, 0, 1) - v_here)
    )
    u_star = wet_x * (u_here - DTDX * adv_u) / (1.0 + FRIC * jnp.abs(u_here))
    v_star = wet_y * (v_here - DTDX * adv_v) / (1.0 + FRIC * jnp.abs(v_here))
    return (
        u_star,
        v_star,
        wet_x,
        wet_y,
        CK * depth_x * wet_x,
        CK * depth_y * wet_y,
        depth_x * u_star,
        depth_y * v_star,
    )


def inner(a):
    return a[:, 1:-1, 1:-1]


def right_side(eta, rain, flux_x, flux_y):
    div = inner(flux_x) - flux_x[:, 1:-1, :-2] + (inner(flux_y) - flux_y[:, :-2, 1:-1])
    return eta + rain - DTDX * div


def operate(e_pad, coef_x, coef_y):
    e_mid = inner(e_pad)
    out = (
        e_mid
        + inner(coef_x) * (e_mid - e_pad[:, 1:-1, 2:])
        + coef_x[:, 1:-1, :-2] * (e_mid - e_pad[:, 1:-1, :-2])
    )
    return (
        out
        + inner(coef_y) * (e_mid - e_pad[:, 2:, 1:-1])
        + coef_y[:, :-2, 1:-1] * (e_mid - e_pad[:, :-2, 1:-1])
    )


def field_pad(field):
    return extended(field, (("row", 1), ("col", 2)), 1)


def squares(residual):
    return lax.psum(jnp.sum(residual * residual, axis=(1, 2)), ("row", "col"))


def spread(values):
    return values[:, None, None]


def body(surface, u_face, v_face, bed_depth, wet_mask, rainfall):
    rows = surface.shape[1]
    cols = surface.shape[2]
    stacked = jnp.stack(
        [
            surface,
            u_face,
            v_face,
            jnp.broadcast_to(bed_depth[None], surface.shape),
            wet_mask.astype(jnp.float32),
        ]
    )
    padded = extended(stacked, (("row", 2), ("col", 3)), 2)
    u_star, v_star, wet_x, wet_y, coef_x, coef_y, flux_x, flux_y = explicit(
        padded[0], padded[1], padded[2], padded[3], padded[4], rows, cols
    )
    rhs = right_side(surface, rainfall, flux_x, flux_y)
    start_pad = padded[0][:, 1:-1, 1:-1]
    solution = surface
    residual = rhs - operate(start_pad, coef_x, coef_y)
    direction = residual
    norm_now = squares(residual)
    for step in range(ITERS):
        direction_pad = field_pad(direction)
        image = operate(direction_pad, coef_x, coef_y)
        alpha = norm_now / lax.psum(jnp.sum(direction * image, axis=(1, 2)), ("row", "col"))
        solution = solution + spread(alpha) * direction
        residual = residual - spread(alpha) * image
        norm_next = squares(residual)
        direction = residual + spread(norm_next / norm_now) * direction
        norm_now = norm_next
    east_col = passed_along(solution[:, :, :1], "col", -1)
    north_row = passed_along(solution[:, :1, :], "row", -1)
    east_field = jnp.concatenate([solution[:, :, 1:], east_col], axis=2)
    north_field = jnp.concatenate([solution[:, 1:, :], north_row], axis=1)
    new_u = inner(u_star) - G1 * inner(wet_x) * (east_field - solution)
    new_v = inner(v_star) - G1 * inner(wet_y) * (north_field - solution)
    return (solution, new_u, new_v)


def solution(mesh):
    in_specs = (
        P(None, "row", "col"),
        P(None, "row", "col"),
        P(None, "row", "col"),
        P("row", "col"),
        P(None, "row", "col"),
        P(None, "row", "col"),
    )
    out_specs = (P(None, "row", "col"), P(None, "row", "col"), P(None, "row", "col"))
    return jax.shard_map(body, mesh=mesh, in_specs=in_specs, out_specs=out_specs, check_vma=False)
```

profile of v0, /device:TPU:14, one launch (start us, length us, event | category | flops | bytes accessed | tf_op | source)
XLA Modules:
  0.0 589.8 jit_solution(1745346275453686401)
XLA Ops:
  4.0 1.9 collective-permute-start
  5.9 3.6 collective-permute-start.1
  11.1 4.2 collective-permute-start.2
  15.3 1.9 collective-permute-start.3
  17.3 6.6 %collective-permute-done.2 = f32[5,2,68,2]{3,2,1,0:T(8,128)S(1)} collective-permute-done((f32[5,2,68,2]{3,2,1,0:T(8,128)S(1)}, f32[5,2,68,2]{3,2,1,0:T(8,128)S(1)}, u32[]{:S(2)}, u32[]{:S(2)}) %collective-permute-start.2) | collective-permute-done | bytes 5472 | tf_op jit(solution)/shard_map/ppermute | solution.py:21
  23.8 6.6 %collective-permute-done.3 = f32[5,2,68,2]{3,2,1,0:T(8,128)S(1)} collective-permute-done((f32[5,2,68,2]{3,2,1,0:T(8,128)S(1)}, f32[5,2,68,2]{3,2,1,0:T(8,128)S(1)}, u32[]{:S(2)}, u32[]{:S(2)}) %collective-permute-start.3) | collective-permute-done | bytes 5472 | tf_op jit(solution)/shard_map/ppermute | solution.py:23
  34.8 2.4 collective-permute-start.4
  37.3 2.5 collective-permute-done.4
  41.7 6.0 %collective-permute-start.7 = (f32[2,66,1]{2,1,0:T(8,128)S(1)}, f32[2,66,1]{2,1,0:T(8,128)S(1)}, u32[]{:S(2)}, u32[]{:S(2)}) collective-permute-start(f32[2,66,1]{2,1,0:T(8,128)S(1)} %get-tuple-element.39), channel_id=1, source_target_pairs={{0,1},{1,2},{2,3},{3,4},{4,5},{5,6},{6,7},{7,8},{8,9},{9,10},{10,1... | collective-permute-start | bytes 1592 | tf_op jit(solution)/shard_map/ppermute | solution.py:21
  50.0 105.9 %all-reduce = (f32[2]{0:T(128)S(1)}, f32[2]{0:T(128)S(1)}) all-reduce(f32[2]{0:T(128)S(1)} %get-tuple-element.4, f32[2]{0:T(128)S(1)} %get-tuple-element.3), channel_id=1, replica_groups=mesh['row'=16,'col'=32] {'row','col'}, use_global_device_ids=true, to_apply=%region_1.2 | all-reduce | flops 4 | bytes 32 | tf_op jit(solution)/shard_map/psum | solution.py:106
  156.1 94.5 %psum.44 = f32[2]{0:T(128)S(1)} all-reduce(f32[2]{0:T(128)S(1)} %get-tuple-element.9), channel_id=1, replica_groups=mesh['row'=16,'col'=32] {'row','col'}, use_global_device_ids=true, to_apply=%region_5.6 | all-reduce | flops 2 | bytes 16 | tf_op jit(solution)/shard_map/psum | solution.py:106
  252.6 2.4 collective-permute-start.8
  255.1 2.5 collective-permute-done.8
  257.6 2.2 collective-permute-start.10
  259.8 5.8 collective-permute-start.11
  267.8 99.5 %psum.45 = f32[2]{0:T(128)S(1)} all-reduce(f32[2]{0:T(128)S(1)} %get-tuple-element.7), channel_id=1, replica_groups=mesh['row'=16,'col'=32] {'row','col'}, use_global_device_ids=true, to_apply=%region_7.8 | all-reduce | flops 2 | bytes 16 | tf_op jit(solution)/shard_map/psum | solution.py:138
  367.5 94.4 %psum.46 = f32[2]{0:T(128)S(1)} all-reduce(f32[2]{0:T(128)S(1)} %multiply_reduce_fusion), channel_id=1, replica_groups=mesh['row'=16,'col'=32] {'row','col'}, use_global_device_ids=true, to_apply=%region_9.10 | all-reduce | flops 2 | bytes 16 | tf_op jit(solution)/shard_map/psum | solution.py:106
  461.9 1.9 collective-permute-start.13
  463.9 2.4 collective-permute-start.12
  466.3 2.5 collective-permute-done.12
  468.8 2.2 collective-permute-start.14
  471.1 5.7 collective-permute-start.15
  479.0 99.4 %psum.47 = f32[2]{0:T(128)S(1)} all-reduce(f32[2]{0:T(128)S(1)} %fusion.28), channel_id=1, replica_groups=mesh['row'=16,'col'=32] {'row','col'}, use_global_device_ids=true, to_apply=%region_11.12 | all-reduce | flops 2 | bytes 16 | tf_op jit(solution)/shard_map/psum | solution.py:138
  582.5 6.5 %collective-permute-done.16 = f32[2,64,1]{2,1,0:T(8,128)S(1)} collective-permute-done((f32[2,64,1]{2,1,0:T(8,128)S(1)}, f32[2,64,1]{2,1,0:T(8,128)S(1)}, u32[]{:S(2)}, u32[]{:S(2)}) %collective-permute-start.16) | collective-permute-done | bytes 544 | tf_op jit(solution)/shard_map/ppermute | solution.py:33
  (71 shorter events, 25.4 us)
Async XLA Ops:
  0.6 0.9 copy-start.3
  1.5 0.8 copy-start.4
  3.1 0.8 copy-start.5
  4.0 5.6 collective-permute-start
  5.9 5.0 collective-permute-start.1
  11.1 12.7 %collective-permute-start.2 = (f32[5,2,68,2]{3,2,1,0:T(8,128)S(1)}, f32[5,2,68,2]{3,2,1,0:T(8,128)S(1)}, u32[]{:S(2)}, u32[]{:S(2)}) collective-permute-start(f32[5,2,68,2]{3,2,1,0:T(8,128)S(1)} %get-tuple-element.30), channel_id=1, source_target_pairs={{0,1},{1,2},{2,3},{3,4},{4,5},{5,6},{6,7},{7,8},{8,9},{9,10},{10,1... | collective-permute-start | bytes 16328 | tf_op jit(solution)/shard_map/ppermute | solution.py:21
  15.3 15.1 %collective-permute-start.3 = (f32[5,2,68,2]{3,2,1,0:T(8,128)S(1)}, f32[5,2,68,2]{3,2,1,0:T(8,128)S(1)}, u32[]{:S(2)}, u32[]{:S(2)}) collective-permute-start(f32[5,2,68,2]{3,2,1,0:T(8,128)S(1)} %get-tuple-element.31), channel_id=1, source_target_pairs={{1,0},{2,1},{3,2},{4,3},{5,4},{6,5},{7,6},{8,7},{9,8},{10,9},{11,1... | collective-permute-start | bytes 16328 | tf_op jit(solution)/shard_map/ppermute | solution.py:23
  31.8 0.8 copy-start.1
  31.8 0.9 copy-start.2
  32.9 4.3 collective-permute-start.5
  34.8 4.9 collective-permute-start.4
  39.8 8.4 %collective-permute-start.6 = (f32[2,66,1]{2,1,0:T(8,128)S(1)}, f32[2,66,1]{2,1,0:T(8,128)S(1)}, u32[]{:S(2)}, u32[]{:S(2)}) collective-permute-start(f32[2,66,1]{2,1,0:T(8,128)S(1)} %get-tuple-element.38), channel_id=1, source_target_pairs={{1,0},{2,1},{3,2},{4,3},{5,4},{6,5},{7,6},{8,7},{9,8},{10,9},{11,1... | collective-permute-start | bytes 1592 | tf_op jit(solution)/shard_map/ppermute | solution.py:23
  41.7 8.0 %collective-permute-start.7 = (f32[2,66,1]{2,1,0:T(8,128)S(1)}, f32[2,66,1]{2,1,0:T(8,128)S(1)}, u32[]{:S(2)}, u32[]{:S(2)}) collective-permute-start(f32[2,66,1]{2,1,0:T(8,128)S(1)} %get-tuple-element.39), channel_id=1, source_target_pairs={{0,1},{1,2},{2,3},{3,4},{4,5},{5,6},{6,7},{7,8},{8,9},{9,10},{10,1... | collective-permute-start | bytes 1592 | tf_op jit(solution)/shard_map/ppermute | solution.py:21
  250.7 4.3 collective-permute-start.9
  252.6 4.9 collective-permute-start.8
  257.6 8.4 %collective-permute-start.10 = (f32[2,66,1]{2,1,0:T(8,128)S(1)}, f32[2,66,1]{2,1,0:T(8,128)S(1)}, u32[]{:S(2)}, u32[]{:S(2)}) collective-permute-start(f32[2,66,1]{2,1,0:T(8,128)S(1)} %get-tuple-element.36), channel_id=1, source_target_pairs={{1,0},{2,1},{3,2},{4,3},{5,4},{6,5},{7,6},{8,7},{9,8},{10,9},{11,1... | collective-permute-start | bytes 1592 | tf_op jit(solution)/shard_map/ppermute | solution.py:23
  259.8 7.7 %collective-permute-start.11 = (f32[2,66,1]{2,1,0:T(8,128)S(1)}, f32[2,66,1]{2,1,0:T(8,128)S(1)}, u32[]{:S(2)}, u32[]{:S(2)}) collective-permute-start(f32[2,66,1]{2,1,0:T(8,128)S(1)} %get-tuple-element.37), channel_id=1, source_target_pairs={{0,1},{1,2},{2,3},{3,4},{4,5},{5,6},{6,7},{7,8},{8,9},{9,10},{10,1... | collective-permute-start | bytes 1592 | tf_op jit(solution)/shard_map/ppermute | solution.py:21
  461.9 4.3 collective-permute-start.13
  463.9 4.9 collective-permute-start.12
  468.8 8.4 %collective-permute-start.14 = (f32[2,66,1]{2,1,0:T(8,128)S(1)}, f32[2,66,1]{2,1,0:T(8,128)S(1)}, u32[]{:S(2)}, u32[]{:S(2)}) collective-permute-start(f32[2,66,1]{2,1,0:T(8,128)S(1)} %get-tuple-element.34), channel_id=1, source_target_pairs={{1,0},{2,1},{3,2},{4,3},{5,4},{6,5},{7,6},{8,7},{9,8},{10,9},{11,1... | collective-permute-start | bytes 1592 | tf_op jit(solution)/shard_map/ppermute | solution.py:23
  471.1 7.7 %collective-permute-start.15 = (f32[2,66,1]{2,1,0:T(8,128)S(1)}, f32[2,66,1]{2,1,0:T(8,128)S(1)}, u32[]{:S(2)}, u32[]{:S(2)}) collective-permute-start(f32[2,66,1]{2,1,0:T(8,128)S(1)} %get-tuple-element.35), channel_id=1, source_target_pairs={{0,1},{1,2},{2,3},{3,4},{4,5},{5,6},{6,7},{7,8},{8,9},{9,10},{10,1... | collective-permute-start | bytes 1592 | tf_op jit(solution)/shard_map/ppermute | solution.py:21
  578.5 10.5 %copy-start = (f32[2,64,128]{2,1,0:T(8,128)}, f32[2,64,128]{2,1,0:T(8,128)S(1)}, u32[]{:S(2)}) copy-start(f32[2,64,128]{2,1,0:T(8,128)S(1)} %multiply_add_fusion) | copy-start | bytes 196612
  578.5 10.4 %collective-permute-start.17 = (f32[2,1,128]{2,1,0:T(1,128)S(1)}, f32[2,1,128]{2,1,0:T(1,128)S(1)}, u32[]{:S(2)}, u32[]{:S(2)}) collective-permute-start(f32[2,1,128]{2,1,0:T(1,128)S(1)} %slice.398), channel_id=1, source_target_pairs={{32,0},{64,32},{96,64},{128,96},{160,128},{192,160},{224,192},{256... | collective-permute-start | bytes 3080 | tf_op jit(solution)/shard_map/ppermute | solution.py:33
  580.5 8.5 %collective-permute-start.16 = (f32[2,64,1]{2,1,0:T(8,128)S(1)}, f32[2,64,1]{2,1,0:T(8,128)S(1)}, u32[]{:S(2)}, u32[]{:S(2)}) collective-permute-start(f32[2,64,1]{2,1,0:T(8,128)S(1)} %bitcast.19), channel_id=1, source_target_pairs={{1,0},{2,1},{3,2},{4,3},{5,4},{6,5},{7,6},{8,7},{9,8},{10,9},{11,1... | collective-permute-start | bytes 1544 | tf_op jit(solution)/shard_map/ppermute | solution.py:33
  (1 other events, 0.8 us)
where the time goes:
time: 591 us; the launch traced here: 590 us
  blocking collectives  494 us (84%)
  starting transfers between devices  52.3 us (9%)
  waiting for transfers between devices  34.3 us (6%)
    psum x3, blocking collectives, squares(): return lax.psum(jnp.sum(residual * residual, axis=(1, 2)), ('row', 'col'))  295 us
    psum x2, blocking collectives, body(): lax.psum(jnp.sum(direction * image, axis=(1, 2)), ('row', 'col'))  199 us
    ppermute x8, starting transfers between devices, extended(): lax.ppermute(tail, axis, [(i, (i + 1) % count) for i in range(ends)])  30.9 us
    ppermute x8, waiting for transfers between devices, extended(): lax.ppermute(tail, axis, [(i, (i + 1) % count) for i in range(ends)])  18.7 us
    ppermute x8, starting transfers between devices, extended(): lax.ppermute(head, axis, [((i + 1) % count, i) for i in range(ends)])  17.6 us
  transfers between devices with their start and end apart: 18, of which 13 were waited for; matrix products, arithmetic and copies ran while one was open for 0% of the time, Pallas kernels for 0%

commit v1 on v0

--- a/solution.py
+++ b/solution.py
@@ -103,7 +103,7 @@
 
 
 def squares(residual):
-    return lax.psum(jnp.sum(residual * residual, axis=(1, 2)), ("row", "col"))
+    return jax.lax.psum(jax.lax.psum(jnp.sum(residual * residual, axis=(1, 2)), "row"), "col")
 
 
 def spread(values):

time: 591 us -> 683 us (1.16)
  blocking collectives: 494 us -> 579 us
    psum x2 -> x3, blocking collectives: 199 us -> 309 us  [body(): lax.psum(jnp.sum(direction * image, axis=(1, 2)), ('row', 'col'))]
    psum x3 -> x6, blocking collectives: 295 us -> 270 us  [the longest x3 206 us: squares(): jax.lax.psum(jax.lax.psum(jnp.sum(residual * residual, axis=(1, 2)), 'row...]
where the time goes in v1:
time: 683 us; the launch traced here: 682 us
  blocking collectives  579 us (85%)
  starting transfers between devices  52.3 us (8%)
  waiting for transfers between devices  41.1 us (6%)
    psum x3, blocking collectives, body(): lax.psum(jnp.sum(direction * image, axis=(1, 2)), ('row', 'col'))  309 us
    psum x3, blocking collectives, squares(): jax.lax.psum(jax.lax.psum(jnp.sum(residual * residual, axis=(1, 2)), 'row...  206 us
    psum x3, blocking collectives, squares(): jax.lax.psum(jnp.sum(residual * residual, axis=(1, 2)), 'row')  64.5 us
    ppermute x8, starting transfers between devices, extended(): lax.ppermute(tail, axis, [(i, (i + 1) % count) for i in range(ends)])  29.4 us
    ppermute x8, waiting for transfers between devices, extended(): lax.ppermute(tail, axis, [(i, (i + 1) % count) for i in range(ends)])  25.5 us
    ppermute x8, starting transfers between devices, extended(): lax.ppermute(head, axis, [((i + 1) % count, i) for i in range(ends)])  19.2 us
  transfers between devices with their start and end apart: 18, of which 13 were waited for; matrix products, arithmetic and copies ran while one was open for 0% of the time, Pallas kernels for 0%

profile of v1, /device:TPU:14, one launch (start us, length us, event | category | flops | bytes accessed | tf_op | source)
XLA Modules:
  0.0 682.1 jit_solution(3120193788076422963)
XLA Ops:
  5.9 3.6 collective-permute-start.1
  11.1 4.2 collective-permute-start.2
  17.3 6.6 collective-permute-done.2
  23.8 6.6 collective-permute-done.3
  34.8 2.4 collective-permute-start.4
  37.3 2.5 collective-permute-done.4
  41.7 6.0 collective-permute-start.7
  50.0 21.1 %psum.63 = f32[2]{0:T(128)S(1)} all-reduce(f32[2]{0:T(128)S(1)} %get-tuple-element.4), channel_id=1, replica_groups=mesh['row'=16,'col'=32] {'row'}, use_global_device_ids=true, to_apply=%region_1.2 | all-reduce | flops 2 | bytes 16 | tf_op jit(solution)/shard_map/psum | solution.py:106
  71.1 108.7 %psum.65 = f32[2]{0:T(128)S(1)} all-reduce(f32[2]{0:T(128)S(1)} %get-tuple-element.3), channel_id=1, replica_groups=mesh['row'=16,'col'=32] {'row','col'}, use_global_device_ids=true, to_apply=%region_4.5 | all-reduce | flops 2 | bytes 16 | tf_op jit(solution)/shard_map/psum | solution.py:138
  179.8 66.8 %psum.64 = f32[2]{0:T(128)S(1)} all-reduce(f32[2]{0:T(128)S(1)} %psum.63), channel_id=1, replica_groups=mesh['row'=16,'col'=32] {'col'}, use_global_device_ids=true, to_apply=%region_2.3 | all-reduce | flops 2 | bytes 16 | tf_op jit(solution)/shard_map/psum | solution.py:106
  246.8 21.4 %psum.66 = f32[2]{0:T(128)S(1)} all-reduce(f32[2]{0:T(128)S(1)} %get-tuple-element.7), channel_id=1, replica_groups=mesh['row'=16,'col'=32] {'row'}, use_global_device_ids=true, to_apply=%region_6.7 | all-reduce | flops 2 | bytes 16 | tf_op jit(solution)/shard_map/psum | solution.py:106
  268.3 71.9 %psum.67 = f32[2]{0:T(128)S(1)} all-reduce(f32[2]{0:T(128)S(1)} %psum.66), channel_id=1, replica_groups=mesh['row'=16,'col'=32] {'col'}, use_global_device_ids=true, to_apply=%region_7.8 | all-reduce | flops 2 | bytes 16 | tf_op jit(solution)/shard_map/psum | solution.py:106
  344.6 4.3 collective-permute-done.8
  351.0 6.0 collective-permute-start.11
  357.4 3.1 collective-permute-done.11
  360.8 100.1 %psum.68 = f32[2]{0:T(128)S(1)} all-reduce(f32[2]{0:T(128)S(1)} %get-tuple-element.5), channel_id=1, replica_groups=mesh['row'=16,'col'=32] {'row','col'}, use_global_device_ids=true, to_apply=%region_9.10 | all-reduce | flops 2 | bytes 16 | tf_op jit(solution)/shard_map/psum | solution.py:138
  461.1 21.9 %psum.69 = f32[2]{0:T(128)S(1)} all-reduce(f32[2]{0:T(128)S(1)} %multiply_reduce_fusion), channel_id=1, replica_groups=mesh['row'=16,'col'=32] {'row'}, use_global_device_ids=true, to_apply=%region_11.12 | all-reduce | flops 2 | bytes 16 | tf_op jit(solution)/shard_map/psum | solution.py:106
  483.0 66.8 %psum.70 = f32[2]{0:T(128)S(1)} all-reduce(f32[2]{0:T(128)S(1)} %psum.69), channel_id=1, replica_groups=mesh['row'=16,'col'=32] {'col'}, use_global_device_ids=true, to_apply=%region_12.13 | all-reduce | flops 2 | bytes 16 | tf_op jit(solution)/shard_map/psum | solution.py:106
  554.3 4.3 collective-permute-done.12
  558.7 4.0 collective-permute-start.14
  562.7 4.0 collective-permute-start.15
  567.1 3.1 collective-permute-done.15
  570.5 100.2 %psum.71 = f32[2]{0:T(128)S(1)} all-reduce(f32[2]{0:T(128)S(1)} %fusion.28), channel_id=1, replica_groups=mesh['row'=16,'col'=32] {'row','col'}, use_global_device_ids=true, to_apply=%region_14.15 | all-reduce | flops 2 | bytes 16 | tf_op jit(solution)/shard_map/psum | solution.py:138
  674.8 6.5 collective-permute-done.16
  (75 shorter events, 34.7 us)
Async XLA Ops:
  0.6 0.9 copy-start.3
  1.5 0.8 copy-start.4
  3.1 0.8 copy-start.5
  4.0 5.6 collective-permute-start
  5.9 5.0 collective-permute-start.1
  11.1 12.7 %collective-permute-start.2 = (f32[5,2,68,2]{3,2,1,0:T(8,128)S(1)}, f32[5,2,68,2]{3,2,1,0:T(8,128)S(1)}, u32[]{:S(2)}, u32[]{:S(2)}) collective-permute-start(f32[5,2,68,2]{3,2,1,0:T(8,128)S(1)} %get-tuple-element.28), channel_id=1, source_target_pairs={{0,1},{1,2},{2,3},{3,4},{4,5},{5,6},{6,7},{7,8},{8,9},{9,10},{10,1... | collective-permute-start | bytes 16328 | tf_op jit(solution)/shard_map/ppermute | solution.py:21
  15.3 15.1 %collective-permute-start.3 = (f32[5,2,68,2]{3,2,1,0:T(8,128)S(1)}, f32[5,2,68,2]{3,2,1,0:T(8,128)S(1)}, u32[]{:S(2)}, u32[]{:S(2)}) collective-permute-start(f32[5,2,68,2]{3,2,1,0:T(8,128)S(1)} %get-tuple-element.29), channel_id=1, source_target_pairs={{1,0},{2,1},{3,2},{4,3},{5,4},{6,5},{7,6},{8,7},{9,8},{10,9},{11,1... | collective-permute-start | bytes 16328 | tf_op jit(solution)/shard_map/ppermute | solution.py:23
  31.8 0.8 copy-start.1
  31.8 0.9 copy-start.2
  32.9 4.3 collective-permute-start.5
  34.8 4.9 collective-permute-start.4
  39.8 8.4 %collective-permute-start.6 = (f32[2,66,1]{2,1,0:T(8,128)S(1)}, f32[2,66,1]{2,1,0:T(8,128)S(1)}, u32[]{:S(2)}, u32[]{:S(2)}) collective-permute-start(f32[2,66,1]{2,1,0:T(8,128)S(1)} %get-tuple-element.36), channel_id=1, source_target_pairs={{1,0},{2,1},{3,2},{4,3},{5,4},{6,5},{7,6},{8,7},{9,8},{10,9},{11,1... | collective-permute-start | bytes 1592 | tf_op jit(solution)/shard_map/ppermute | solution.py:23
  41.7 8.0 %collective-permute-start.7 = (f32[2,66,1]{2,1,0:T(8,128)S(1)}, f32[2,66,1]{2,1,0:T(8,128)S(1)}, u32[]{:S(2)}, u32[]{:S(2)}) collective-permute-start(f32[2,66,1]{2,1,0:T(8,128)S(1)} %get-tuple-element.37), channel_id=1, source_target_pairs={{0,1},{1,2},{2,3},{3,4},{4,5},{5,6},{6,7},{7,8},{8,9},{9,10},{10,1... | collective-permute-start | bytes 1592 | tf_op jit(solution)/shard_map/ppermute | solution.py:21
  340.3 4.3 collective-permute-start.9
  342.2 6.7 collective-permute-start.8
  349.0 8.4 %collective-permute-start.10 = (f32[2,66,1]{2,1,0:T(8,128)S(1)}, f32[2,66,1]{2,1,0:T(8,128)S(1)}, u32[]{:S(2)}, u32[]{:S(2)}) collective-permute-start(f32[2,66,1]{2,1,0:T(8,128)S(1)} %get-tuple-element.34), channel_id=1, source_target_pairs={{1,0},{2,1},{3,2},{4,3},{5,4},{6,5},{7,6},{8,7},{9,8},{10,9},{11,1... | collective-permute-start | bytes 1592 | tf_op jit(solution)/shard_map/ppermute | solution.py:23
  351.0 9.6 %collective-permute-start.11 = (f32[2,66,1]{2,1,0:T(8,128)S(1)}, f32[2,66,1]{2,1,0:T(8,128)S(1)}, u32[]{:S(2)}, u32[]{:S(2)}) collective-permute-start(f32[2,66,1]{2,1,0:T(8,128)S(1)} %get-tuple-element.35), channel_id=1, source_target_pairs={{0,1},{1,2},{2,3},{3,4},{4,5},{5,6},{6,7},{7,8},{8,9},{9,10},{10,1... | collective-permute-start | bytes 1592 | tf_op jit(solution)/shard_map/ppermute | solution.py:21
  549.9 4.3 collective-permute-start.13
  551.9 6.7 collective-permute-start.12
  558.7 8.4 %collective-permute-start.14 = (f32[2,66,1]{2,1,0:T(8,128)S(1)}, f32[2,66,1]{2,1,0:T(8,128)S(1)}, u32[]{:S(2)}, u32[]{:S(2)}) collective-permute-start(f32[2,66,1]{2,1,0:T(8,128)S(1)} %get-tuple-element.32), channel_id=1, source_target_pairs={{1,0},{2,1},{3,2},{4,3},{5,4},{6,5},{7,6},{8,7},{9,8},{10,9},{11,1... | collective-permute-start | bytes 1592 | tf_op jit(solution)/shard_map/ppermute | solution.py:23
  562.7 7.5 %collective-permute-start.15 = (f32[2,66,1]{2,1,0:T(8,128)S(1)}, f32[2,66,1]{2,1,0:T(8,128)S(1)}, u32[]{:S(2)}, u32[]{:S(2)}) collective-permute-start(f32[2,66,1]{2,1,0:T(8,128)S(1)} %get-tuple-element.33), channel_id=1, source_target_pairs={{0,1},{1,2},{2,3},{3,4},{4,5},{5,6},{6,7},{7,8},{8,9},{9,10},{10,1... | collective-permute-start | bytes 1592 | tf_op jit(solution)/shard_map/ppermute | solution.py:21
  670.8 10.5 %copy-start = (f32[2,64,128]{2,1,0:T(8,128)}, f32[2,64,128]{2,1,0:T(8,128)S(1)}, u32[]{:S(2)}) copy-start(f32[2,64,128]{2,1,0:T(8,128)S(1)} %multiply_add_fusion) | copy-start | bytes 196612
  670.8 10.4 %collective-permute-start.17 = (f32[2,1,128]{2,1,0:T(1,128)S(1)}, f32[2,1,128]{2,1,0:T(1,128)S(1)}, u32[]{:S(2)}, u32[]{:S(2)}) collective-permute-start(f32[2,1,128]{2,1,0:T(1,128)S(1)} %slice.398), channel_id=1, source_target_pairs={{32,0},{64,32},{96,64},{128,96},{160,128},{192,160},{224,192},{256... | collective-permute-start | bytes 3080 | tf_op jit(solution)/shard_map/ppermute | solution.py:33
  672.7 8.5 %collective-permute-start.16 = (f32[2,64,1]{2,1,0:T(8,128)S(1)}, f32[2,64,1]{2,1,0:T(8,128)S(1)}, u32[]{:S(2)}, u32[]{:S(2)}) collective-permute-start(f32[2,64,1]{2,1,0:T(8,128)S(1)} %bitcast.19), channel_id=1, source_target_pairs={{1,0},{2,1},{3,2},{4,3},{5,4},{6,5},{7,6},{8,7},{9,8},{10,9},{11,1... | collective-permute-start | bytes 1544 | tf_op jit(solution)/shard_map/ppermute | solution.py:33
  (1 other events, 0.8 us)
